TPU v7x, 128 devices: a whole 4x4x4 slice. The times are simulated.
128 devices in a mesh: req: 16 (over y_lo, z, core), tp: 8 (over y_hi, x).
Axes of the slice: x: 4, y: 4 (y_hi: 2, y_lo: 2; y = y_hi * 2 + y_lo), z: 4, core: 2. Of those that a mesh axis runs over, the one named last changes fastest.
Arguments:
- tokens: bfloat16 [2048, 2048], P('req')
- attn_gain: float32 [2048], replicated, may hold values from 0.25 to 1.75
- query_gain: float32 [128], replicated, may hold values from 0.8 to 2
- key_gain: float32 [128], replicated, may hold values from 0.8 to 2
- moe_gain: float32 [2048], replicated, may hold values from 0.25 to 1.75
- query_weight: float32 [2048, 2048], P('req', 'tp'), may hold values from -0.125 to 0.125
- key_weight: float32 [2048, 2048], P('req', 'tp'), may hold values from -0.125 to 0.125
- value_weight: float32 [2048, 2048], P('req', 'tp'), may hold values from -0.125 to 0.125
- out_weight: float32 [2048, 2048], P('tp', 'req'), may hold values from -0.125 to 0.125
- gate_weight: float32 [64, 2048, 1024], P(None, ('req', 'tp')), may hold values from -0.125 to 0.125
- up_weight: float32 [64, 2048, 1024], P(None, ('req', 'tp')), may hold values from -0.125 to 0.125
- down_weight: bfloat16 [128, 512, 2048], P(('req', 'tp')), may hold values from -0.1875 to 0.1875
- router_weight: bfloat16 [2048, 64], replicated, may hold values from -0.125 to 0.125
- page_store: bfloat16 [128, 128, 2, 2048], P('req', None, None, 'tp'), may hold values from -3 to 3
- prompt_lengths: int32 [32], replicated, may hold values from 32 to 96, as said below
- continues: int32 [32], replicated, may hold values from 0 to 1, as said below
- page_owner: int32 [16, 16], replicated, may hold values from 0 to 15, as said below
- page_slot: int32 [16, 16], replicated, may hold values from 0 to 7
- routes: int32 [2048, 8], P(('req', 'tp')), may hold values from 0 to 63, as said below
Outputs:
- server_qkv: bfloat16 [2048, 6144], P(None, 'tp')
- server_out: bfloat16 [2048, 2048], P('tp')
- server_gate_up: bfloat16 [128, 2048, 1024], P(('req', 'tp'))
- hidden: bfloat16 [2048, 2048], P(('req', 'tp'))
- new_cache: bfloat16 [2048, 2, 2048], P('req', None, 'tp')
Inputs may be any that keep to these rules, and one draw needn't show every extreme that they name: `prompt_lengths`: entries 2g and 2g + 1 are the two prompt lengths of group g and sum to 128. Exactly one of the two prompts of each group continues an earlier request. `page_owner`: no page of group g lies on g itself; at most 2 of a group's 16 pages lie on one owner, and every group has exactly 2 pages on some owner. `routes`: each row names 8 different experts. In each aligned block of 16 rows (the rows of one device) no expert is named by more than 3 rows, and one expert, the same in every block, is named by exactly 3 rows in each block.
All inputs are finite; a program needn't handle non-finite values.
Results may differ from a plain program's by a relative error of at most 0.0057.
Values may be sent and summed in bfloat16 or wider, within the bound.
A program may use at most 128 MiB of HBM per device.

v0:
```python
import math
import jax
import jax.numpy as jnp
from jax import lax
from jax.sharding import PartitionSpec as P

norm_eps = 1e-06
rope_base = 50000.0


def rms_scale(values, gain_vec):
    return (
        values * lax.rsqrt(jnp.mean(values * values, axis=-1, keepdims=True) + norm_eps) * gain_vec
    )


def rotate_half(values, cosine, sine_part):
    half_width = values.shape[-1] // 2
    first_half = values[..., :half_width]
    second_half = values[..., half_width:]
    return jnp.concatenate(
        [
            first_half * cosine - second_half * sine_part,
            second_half * cosine + first_half * sine_part,
        ],
        axis=-1,
    )


def split_halves(weights):
    expert_count, rows_here, hidden_units = weights.shape
    return weights.reshape(expert_count, rows_here, 2, hidden_units // 2).transpose(0, 2, 1, 3)


def body(
    tokens,
    attn_gain,
    query_gain,
    key_gain,
    moe_gain,
    query_weight,
    key_weight,
    value_weight,
    out_weight,
    gate_weight,
    up_weight,
    down_weight,
    router_weight,
    page_store,
    prompt_lengths,
    continues,
    page_owner,
    page_slot,
    routes,
):
    req_count = lax.axis_size("req")
    req_index = lax.axis_index("req")
    lane_index = lax.axis_index("tp")
    joined_local = jnp.concatenate(
        [
            query_weight.astype(jnp.bfloat16),
            key_weight.astype(jnp.bfloat16),
            value_weight.astype(jnp.bfloat16),
        ],
        axis=1,
    )
    server_qkv, server_out = (
        lax.all_gather(joined_local, "req", axis=0, tiled=True),
        lax.all_gather(out_weight.astype(jnp.bfloat16), "req", axis=1, tiled=True),
    )
    expert_count, rows_here, hidden_units = gate_weight.shape
    half_units = hidden_units // 2
    packed = jnp.concatenate(
        [
            split_halves(gate_weight.astype(jnp.bfloat16)),
            split_halves(up_weight.astype(jnp.bfloat16)),
        ],
        axis=3,
    ).reshape(2 * expert_count, rows_here, hidden_units)
    server_gate_up = lax.all_to_all(packed, ("req", "tp"), split_axis=0, concat_axis=1, tiled=True)
    group_rows, model_width = tokens.shape
    tokens_f32 = tokens.astype(jnp.float32)
    normed = rms_scale(tokens_f32, attn_gain).astype(jnp.bfloat16)
    projected = jnp.dot(normed, server_qkv, preferred_element_type=jnp.float32)
    head_dim = query_gain.shape[0]
    lane_width = server_qkv.shape[1] // 3
    lane_heads = lane_width // head_dim
    query_raw = projected[:, :lane_width].reshape(group_rows, lane_heads, head_dim)
    key_raw = projected[:, lane_width : 2 * lane_width].reshape(group_rows, lane_heads, head_dim)
    value_raw = projected[:, 2 * lane_width :]
    first_length = lax.dynamic_index_in_dim(prompt_lengths, 2 * req_index, 0, keepdims=False)
    carry_flags = lax.dynamic_slice_in_dim(continues, 2 * req_index, 2)
    row_ids = jnp.arange(group_rows, dtype=jnp.int32)
    second = (row_ids >= first_length).astype(jnp.int32)
    within = row_ids - second * first_length
    carried = jnp.where(second == 1, carry_flags[1], carry_flags[0])
    pages_per = page_owner.shape[1]
    page_rows = page_store.shape[1]
    context_len = pages_per * page_rows
    position = (within + context_len * carried).astype(jnp.float32)
    inverse = jnp.power(
        jnp.float32(rope_base), -(jnp.arange(head_dim // 2, dtype=jnp.float32) * 2.0 / head_dim)
    )
    angles = position[:, None, None] * inverse[None, None, :]
    cosine = jnp.cos(angles)
    sine_part = jnp.sin(angles)
    query_rows = rotate_half(rms_scale(query_raw, query_gain), cosine, sine_part).astype(
        jnp.bfloat16
    )
    keys_new = rotate_half(rms_scale(key_raw, key_gain), cosine, sine_part).astype(jnp.bfloat16)
    values_new = value_raw.astype(jnp.bfloat16)
    new_cache = jnp.stack([keys_new.reshape(group_rows, lane_width), values_new], axis=1)
    capacity = max(2, (pages_per + req_count - 2) // (req_count - 1))
    page_ids = jnp.arange(pages_per, dtype=jnp.int32)
    earlier = page_ids[None, :] < page_ids[:, None]
    same_owner = page_owner[:, :, None] == page_owner[:, None, :]
    page_rank = jnp.sum((same_owner & earlier[None]).astype(jnp.int32), axis=2)
    owned_here = page_owner == req_index
    chosen = owned_here[:, None, :] & (
        page_rank[:, None, :] == jnp.arange(capacity, dtype=jnp.int32)[None, :, None]
    )
    send_slot = jnp.sum(jnp.where(chosen, page_slot[:, None, :], 0), axis=2)
    send_live = jnp.any(chosen, axis=2)
    page_shape = page_store.shape[1:]
    outgoing_pages = jnp.take(page_store, send_slot.reshape(-1), axis=0).reshape(
        (req_count, capacity) + page_shape
    )
    outgoing_pages = jnp.where(
        send_live[:, :, None, None, None], outgoing_pages, jnp.zeros_like(outgoing_pages)
    )
    arrived_pages = lax.all_to_all(outgoing_pages, "req", split_axis=0, concat_axis=0, tiled=True)
    own_owner = jnp.take(page_owner, req_index, axis=0)
    own_rank = jnp.take(page_rank, req_index, axis=0)
    context = jnp.take(
        arrived_pages.reshape((req_count * capacity,) + page_shape),
        own_owner * capacity + own_rank,
        axis=0,
    )
    context = context.reshape(context_len, 2, lane_heads, head_dim)
    score_scale = 1.0 / math.sqrt(head_dim)
    near_scores = (
        jnp.einsum("ihc,jhc->hij", query_rows, keys_new, preferred_element_type=jnp.float32)
        * score_scale
    )
    far_scores = (
        jnp.einsum("ihc,jhc->hij", query_rows, context[:, 0], preferred_element_type=jnp.float32)
        * score_scale
    )
    same_request = second[:, None] == second[None, :]
    near_weights = jnp.where(same_request[None], jnp.exp(near_scores), jnp.float32(0.0))
    far_weights = jnp.where((carried == 1)[None, :, None], jnp.exp(far_scores), jnp.float32(0.0))
    totals = jnp.sum(near_weights, axis=2, keepdims=True) + jnp.sum(
        far_weights, axis=2, keepdims=True
    )
    near_probs = (near_weights / totals).astype(jnp.bfloat16)
    far_probs = (far_weights / totals).astype(jnp.bfloat16)
    attended = jnp.einsum(
        "hij,jhc->ihc",
        near_probs,
        values_new.reshape(group_rows, lane_heads, head_dim),
        preferred_element_type=jnp.float32,
    )
    attended = attended + jnp.einsum(
        "hij,jhc->ihc", far_probs, context[:, 1], preferred_element_type=jnp.float32
    )
    attended = attended.astype(jnp.bfloat16).reshape(group_rows, lane_width)
    shard_rows = routes.shape[0]
    row_start = lane_index * shard_rows
    head_terms = jnp.dot(attended, server_out, preferred_element_type=jnp.float32)
    mixed_all = lax.psum(head_terms, "tp")
    mixed_own = lax.dynamic_slice_in_dim(mixed_all, row_start, shard_rows, 0)
    residual_own = lax.dynamic_slice_in_dim(tokens_f32, row_start, shard_rows, 0) + mixed_own
    moe_own = rms_scale(residual_own, moe_gain).astype(jnp.bfloat16)
    logits = jnp.dot(moe_own, router_weight, preferred_element_type=jnp.float32)
    exps = jnp.exp(logits)
    routed_exps = jnp.take_along_axis(exps, routes, axis=1)
    entry_gates = routed_exps / jnp.sum(routed_exps, axis=1, keepdims=True)
    top_count = routes.shape[1]
    slot_depth = 3 * shard_rows * top_count // (2 * expert_count)
    flat_routes = routes.reshape(-1)
    onehot = (flat_routes[:, None] == jnp.arange(expert_count, dtype=jnp.int32)[None, :]).astype(
        jnp.int32
    )
    entry_rank = jnp.sum((jnp.cumsum(onehot, axis=0) - onehot) * onehot, axis=1)
    entry_slot = (flat_routes * slot_depth + entry_rank).reshape(shard_rows, top_count)
    select_table = jnp.any(
        entry_slot[None, :, :]
        == jnp.arange(expert_count * slot_depth, dtype=jnp.int32)[:, None, None],
        axis=2,
    ).astype(jnp.bfloat16)
    outgoing_rows = jnp.dot(select_table, moe_own, preferred_element_type=jnp.float32).astype(
        jnp.bfloat16
    )
    send_rows = jnp.broadcast_to(
        outgoing_rows.reshape(expert_count, 1, slot_depth, model_width),
        (expert_count, 2, slot_depth, model_width),
    ).reshape(2 * expert_count, slot_depth, model_width)
    arrived_rows = lax.all_to_all(send_rows, ("req", "tp"), split_axis=0, concat_axis=0, tiled=True)
    flat_rows = arrived_rows.reshape(-1, model_width)
    both = jnp.dot(flat_rows, server_gate_up[0], preferred_element_type=jnp.float32)
    act = (jax.nn.silu(both[:, :half_units]) * both[:, half_units:]).astype(jnp.bfloat16)
    expert_rows = (
        jnp.dot(act, down_weight[0], preferred_element_type=jnp.float32)
        .astype(jnp.bfloat16)
        .reshape(arrived_rows.shape)
    )
    returned = lax.all_to_all(expert_rows, ("req", "tp"), split_axis=0, concat_axis=0, tiled=True)
    returned = returned.reshape(expert_count, 2, slot_depth, model_width)
    joined_out = (returned[:, 0].astype(jnp.float32) + returned[:, 1].astype(jnp.float32)).reshape(
        expert_count * slot_depth, model_width
    )
    picked_rows = jnp.take(joined_out, entry_slot.reshape(-1), axis=0).reshape(
        shard_rows, top_count, model_width
    )
    moe_out = jnp.sum(picked_rows * entry_gates[:, :, None], axis=1)
    hidden_rows = (residual_own + moe_out).astype(jnp.bfloat16)
    return (server_qkv, server_out, server_gate_up, hidden_rows, new_cache)


def solution(mesh):
    in_specs = (
        P("req", None),
        P(),
        P(),
        P(),
        P(),
        P("req", "tp"),
        P("req", "tp"),
        P("req", "tp"),
        P("tp", "req"),
        P(None, ("req", "tp"), None),
        P(None, ("req", "tp"), None),
        P(("req", "tp"), None, None),
        P(),
        P("req", None, None, "tp"),
        P(),
        P(),
        P(),
        P(),
        P(("req", "tp"), None),
    )
    out_specs = (
        P(None, "tp"),
        P("tp", None),
        P(("req", "tp"), None, None),
        P(("req", "tp"), None),
        P("req", None, "tp"),
    )
    return jax.shard_map(body, mesh=mesh, in_specs=in_specs, out_specs=out_specs, check_vma=False)
```

profile of v0, /device:TPU:1, one launch (start us, length us, event | category | flops | bytes accessed | tf_op | source)
XLA Modules:
  0.0 396.9 jit_solution(3636944397927276136)
XLA Ops:
  7.2 1.1 convert_element_type.109
  8.3 0.9 convert_element_type.110
  9.2 0.9 convert_element_type.111
  10.9 1.2 convert_reduce_fusion
  14.1 10.0 %gather_fusion = bf16[32,128,2,256]{3,2,1,0:T(2,128)(2,1)} fusion(bf16[8,128,2,256]{3,2,1,0:T(2,128)(2,1)S(1)} %copy-done.1, s32[1024]{0:T(1024)S(1)} %pad_clamp_fusion.2), kind=kCustom, calls=%fused_computation | custom fusion | bytes 8388736 | tf_op jit(solution)/shard_map/jit(_take)/gather | solution.py:125
  24.2 4.2 %fusion = bf16[16,2,128,2,256]{4,2,3,1,0:T(8,128)(2,1)} fusion(bf16[16,2,128,2,256]{4,3,2,1,0:T(2,128)(2,1)} %bitcast.101, pred[16,2]{1,0:T(8,128)(4,1)S(1)} %copy.132, pred[16,2]{1,0:T(8,128)(4,1)S(1)} %copy.131), kind=kLoop, calls=%fused_computation.6 | loop fusion | flops 4194304 | bytes 8388672 | tf_op jit(solution)/shard_map/jit(_where)/select_n | solution.py:128
  28.4 8.1 %all-to-all-start.1 = ((bf16[16,2,128,2,256]{4,2,3,1,0:T(8,128)(2,1)}), bf16[16,2,128,2,256]{4,2,3,1,0:T(8,128)(2,1)}, u32[]{:S(2)}, u32[]{:S(2)}) async-start(bf16[16,2,128,2,256]{4,2,3,1,0:T(8,128)(2,1)} %fusion), calls=%async_computation.1 | async-start | bytes 8388608 | tf_op jit(solution)/shard_map/all_to_all | solution.py:131
  38.5 1.9 fusion.32
  40.5 1.9 compare_convert_fusion
  43.8 50.5 %all-to-all-done.1 = bf16[16,2,128,2,256]{4,2,3,1,0:T(8,128)(2,1)} async-done(((bf16[16,2,128,2,256]{4,2,3,1,0:T(8,128)(2,1)}), bf16[16,2,128,2,256]{4,2,3,1,0:T(8,128)(2,1)}, u32[]{:S(2)}, u32[]{:S(2)}) %all-to-all-start.1) | async-done | bytes 4194336 | tf_op jit(solution)/shard_map/all_to_all | solution.py:131
  94.4 4.2 %gather_fusion.1 = bf16[16,128,2,256]{3,1,2,0:T(8,128)(2,1)} fusion(bf16[32,128,2,256]{3,1,2,0:T(8,128)(2,1)} %bitcast.13, s32[1024]{0:T(1024)S(1)} %pad_clamp_fusion.1), kind=kCustom, calls=%fused_computation.1 | custom fusion | bytes 4194368 | tf_op jit(solution)/shard_map/jit(_take)/gather | solution.py:134
  98.6 4.5 %copy.135 = bf16[16,128,2,256]{1,0,3,2:T(8,128)(2,1)} copy(bf16[16,128,2,256]{3,1,2,0:T(8,128)(2,1)} %gather_fusion.1) | data formatting | bytes 4194304 | tf_op jit(solution)/shard_map/jit(_take)/gather | solution.py:134
  103.1 4.2 %gather.28 = bf16[2048,2,2,128]{0,3,2,1:T(8,128)(2,1)} reshape(bf16[16,128,2,256]{1,0,3,2:T(8,128)(2,1)} %copy.135) | data formatting | bytes 4194304 | tf_op jit(solution)/shard_map/jit(_take)/gather | solution.py:134
  107.3 4.0 copy.136
  111.2 2.8 broadcast_select_fusion
  114.0 2.5 fusion.11
  119.0 0.8 copy-done.4
  121.3 2.5 fusion.43
  123.9 1.1 convert_element_type.115
  126.0 81.6 %all-reduce.2.cloned.1.call-done = f32[128,2048]{1,0:T(8,128)} async-done(((f32[128,2048]{1,0:T(8,128)}), f32[128,2048]{1,0:T(8,128)}) %all-reduce.2.cloned.1.call-update) | async-done | bytes 1048592 | tf_op jit(solution)/shard_map/psum | solution.py:170
  207.5 1.1 multiply_reduce_fusion.1
  208.6 1.3 convolution_convert_fusion.1
  209.9 2.4 broadcast_in_dim.156
  212.4 2.6 broadcast_in_dim.157
  215.0 11.8 %all-to-all-start.2 = ((bf16[128,3,2048]{2,1,0:T(4,128)(2,1)}), bf16[128,3,2048]{2,1,0:T(4,128)(2,1)}, u32[]{:S(2)}, u32[]{:S(2)}) async-start(bf16[128,3,2048]{2,1,0:T(4,128)(2,1)} %bitcast.102), calls=%async_computation.2 | async-start | bytes 4194304 | tf_op jit(solution)/shard_map/all_to_all | solution.py:198
  226.7 3.8 convert_element_type.113
  230.6 4.5 %reshape.372 = bf16[64,16,2,512]{3,2,1,0:T(2,128)(2,1)} reshape(bf16[64,16,1024]{2,1,0:T(8,128)(2,1)} %convert_element_type.113) | data formatting | bytes 4194304 | tf_op jit(solution)/shard_map/reshape | solution.py:32
  235.1 3.8 convert_element_type.114
  238.9 4.5 %reshape.373 = bf16[64,16,2,512]{3,2,1,0:T(2,128)(2,1)} reshape(bf16[64,16,1024]{2,1,0:T(8,128)(2,1)} %convert_element_type.114) | data formatting | bytes 4194304 | tf_op jit(solution)/shard_map/reshape | solution.py:32
  243.4 10.6 %pad_maximum_fusion = bf16[64,2,16,1024]{3,1,2,0:T(2,128)(2,1)} fusion(bf16[64,2,16,512]{3,1,2,0:T(2,128)(2,1)} %bitcast.104, bf16[64,2,16,512]{3,1,2,0:T(2,128)(2,1)} %bitcast.103), kind=kLoop, calls=%fused_computation.4 | loop fusion | flops 8388608 | bytes 8388608 | tf_op jit(solution)/shard_map/concatenate | solution.py:73
  254.0 5.6 %copy.126 = bf16[64,2,16,1024]{3,2,1,0:T(8,128)(2,1)} copy(bf16[64,2,16,1024]{3,1,2,0:T(2,128)(2,1)} %pad_maximum_fusion) | data formatting | bytes 8388608 | tf_op jit(solution)/shard_map/concatenate | solution.py:73
  259.6 10.2 %all-to-all-start = ((bf16[128,16,1024]{2,1,0:T(8,128)(2,1)}), bf16[128,16,1024]{2,1,0:T(8,128)(2,1)}, u32[]{:S(2)}, u32[]{:S(2)}) async-start(bf16[128,16,1024]{2,1,0:T(8,128)(2,1)} %bitcast.100), calls=%async_computation | async-start | bytes 8388608 | tf_op jit(solution)/shard_map/all_to_all | solution.py:80
  269.8 5.0 %reshape.383 = bf16[384,2048]{1,0:T(8,128)(2,1)} reshape(bf16[128,3,2048]{2,1,0:T(4,128)(2,1)} %all-to-all-done.2) | data formatting | bytes 3145728 | tf_op jit(solution)/shard_map/reshape | solution.py:199
  274.9 46.3 %all-to-all-done = bf16[128,16,1024]{2,1,0:T(8,128)(2,1)} async-done(((bf16[128,16,1024]{2,1,0:T(8,128)(2,1)}), bf16[128,16,1024]{2,1,0:T(8,128)(2,1)}, u32[]{:S(2)}, u32[]{:S(2)}) %all-to-all-start) | async-done | bytes 4194336 | tf_op jit(solution)/shard_map/all_to_all | solution.py:80
  321.1 4.4 %fusion.44 = f32[384,1024]{1,0:T(8,128)S(1)} fusion(bf16[384,2048]{1,0:T(8,128)(2,1)} %reshape.383, bf16[2048,1024]{1,0:T(8,128)(2,1)} %bitcast.19), kind=kOutput, calls=%fused_computation.128 | convolution fusion | flops 1610612736 | bytes 7340032 | tf_op jit(solution)/shard_map/dot_general | solution.py:200
  325.6 2.2 convolution_convert_fusion
  327.8 5.2 %reshape.384 = bf16[128,3,2048]{2,1,0:T(4,128)(2,1)} reshape(bf16[384,2048]{1,0:T(8,128)(2,1)} %convolution_convert_fusion) | data formatting | bytes 3145728 | tf_op jit(solution)/shard_map/reshape | solution.py:205
  332.9 7.4 %all-to-all-start.3 = ((bf16[128,3,2048]{2,1,0:T(4,128)(2,1)}), bf16[128,3,2048]{2,1,0:T(4,128)(2,1)}, u32[]{:S(2)}, u32[]{:S(2)}) async-start(bf16[128,3,2048]{2,1,0:T(4,128)(2,1)} %reshape.384), calls=%async_computation.3 | async-start | bytes 4194304 | tf_op jit(solution)/shard_map/all_to_all | solution.py:207
  341.0 0.9 slice_bitcast_fusion.8
  342.9 1.3 gather_fusion.3
  344.5 24.4 %all-to-all-done.3 = bf16[128,3,2048]{2,1,0:T(4,128)(2,1)} async-done(((bf16[128,3,2048]{2,1,0:T(4,128)(2,1)}), bf16[128,3,2048]{2,1,0:T(4,128)(2,1)}, u32[]{:S(2)}, u32[]{:S(2)}) %all-to-all-start.3) | async-done | bytes 1572896 | tf_op jit(solution)/shard_map/all_to_all | solution.py:207
  368.9 3.7 convert_add_fusion
  372.7 3.8 add.191
  376.4 2.9 gather_fusion.2
  379.3 0.9 fusion.9
  380.9 3.8 copy.168
  384.7 1.0 copy.169
  385.7 4.6 %copy.170 = bf16[1,2048,1024]{2,1,0:T(8,128)(2,1)} copy(bf16[1,2048,1024]{2,1,0:T(8,128)(2,1)} %bitcast.3) | data formatting | bytes 8388608
  (113 shorter events, 13.6 us)
Async XLA Ops:
  7.2 318.4 %copy-start = (bf16[1,512,2048]{2,1,0:T(8,128)(2,1)S(1)}, bf16[1,512,2048]{2,1,0:T(8,128)(2,1)}, u32[]{:S(2)}) copy-start(bf16[1,512,2048]{2,1,0:T(8,128)(2,1)} %param.32) | copy-start | bytes 6291460
  7.2 7.0 %copy-start.1 = (bf16[8,128,2,256]{3,2,1,0:T(2,128)(2,1)S(1)}, bf16[8,128,2,256]{3,2,1,0:T(2,128)(2,1)}, u32[]{:S(2)}) copy-start(bf16[8,128,2,256]{3,2,1,0:T(2,128)(2,1)} %param.34) | copy-start | bytes 3145732
  7.2 106.8 %all-gather.3.cloned.1.call-start = ((), (), s32[]{:S(2)}) async-start(), calls=%async_computation.4 | async-start | bytes 3342336 | tf_op jit(solution)/shard_map/all_gather | solution.py:68
  28.4 8.1 %copy-start.8 = (f32[256,128]{1,0:T(8,128)S(1)}, f32[256,128]{1,0:T(8,128)}, u32[]{:S(2)}) copy-start(f32[256,128]{1,0:T(8,128)} %param.29) | copy-start | bytes 393220
  28.4 8.9 %copy-start.13 = (s32[32]{0:T(128)S(1)}, s32[32]{0:T(128)}, u32[]{:S(2)}) copy-start(s32[32]{0:T(128)} %param.36) | copy-start | bytes 388
  28.4 9.0 %copy-start.14 = (s32[32]{0:T(128)S(1)}, s32[32]{0:T(128)}, u32[]{:S(2)}) copy-start(s32[32]{0:T(128)} %param.35) | copy-start | bytes 388
  28.4 14.8 %copy-start.2 = (bf16[128,2048]{1,0:T(8,128)(2,1)S(1)}, bf16[128,2048]{1,0:T(8,128)(2,1)}, u32[]{:S(2)}) copy-start(bf16[128,2048]{1,0:T(8,128)(2,1)} %param.21) | copy-start | bytes 1572868
  28.4 66.0 %all-to-all-start.1 = ((bf16[16,2,128,2,256]{4,2,3,1,0:T(8,128)(2,1)}), bf16[16,2,128,2,256]{4,2,3,1,0:T(8,128)(2,1)}, u32[]{:S(2)}, u32[]{:S(2)}) async-start(bf16[16,2,128,2,256]{4,2,3,1,0:T(8,128)(2,1)} %fusion), calls=%async_computation.1 | async-start | bytes 8388608 | tf_op jit(solution)/shard_map/all_to_all | solution.py:131
  36.5 84.8 %all-gather.5.cloned.1.call-start = ((), (), s32[]{:S(2)}) async-start(), calls=%async_computation.5 | async-start | bytes 1114112 | tf_op jit(solution)/shard_map/all_gather | solution.py:69
  37.2 170.3 %all-reduce.2.cloned.1.call-start = ((), (), s32[]{:S(2)}) async-start(), calls=%async_computation.6 | async-start | bytes 2097152 | tf_op jit(solution)/shard_map/psum | solution.py:170
  111.2 2.8 copy-start.10
  114.0 4.2 %copy-start.11 = (f32[128]{0:T(128)S(1)}, f32[128]{0:T(128)}, u32[]{:S(2)}) copy-start(f32[128]{0:T(128)} %param.24) | copy-start | bytes 1540
  114.0 4.2 %copy-start.12 = (f32[128]{0:T(128)S(1)}, f32[128]{0:T(128)}, u32[]{:S(2)}) copy-start(f32[128]{0:T(128)} %param.23) | copy-start | bytes 1540
  116.5 0.8 copy-start.5
  118.2 1.6 copy-start.4
  121.3 3.6 copy-start.7
  123.9 84.8 %copy-start.9 = (f32[2048]{0:T(1024)S(1)}, f32[2048]{0:T(1024)}, u32[]{:S(2)}) copy-start(f32[2048]{0:T(1024)} %param.25) | copy-start | bytes 24580
  215.0 44.6 %all-to-all-start.2 = ((bf16[128,3,2048]{2,1,0:T(4,128)(2,1)}), bf16[128,3,2048]{2,1,0:T(4,128)(2,1)}, u32[]{:S(2)}, u32[]{:S(2)}) async-start(bf16[128,3,2048]{2,1,0:T(4,128)(2,1)} %bitcast.102), calls=%async_computation.2 | async-start | bytes 4194304 | tf_op jit(solution)/shard_map/all_to_all | solution.py:198
  259.6 61.5 %all-to-all-start = ((bf16[128,16,1024]{2,1,0:T(8,128)(2,1)}), bf16[128,16,1024]{2,1,0:T(8,128)(2,1)}, u32[]{:S(2)}, u32[]{:S(2)}) async-start(bf16[128,16,1024]{2,1,0:T(8,128)(2,1)} %bitcast.100), calls=%async_computation | async-start | bytes 8388608 | tf_op jit(solution)/shard_map/all_to_all | solution.py:80
  332.9 9.8 %copy-start.6 = (bf16[2048,64]{0,1:T(8,128)(2,1)S(1)}, bf16[2048,64]{0,1:T(8,128)(2,1)}, u32[]{:S(2)}) copy-start(bf16[2048,64]{0,1:T(8,128)(2,1)} %param.33) | copy-start | bytes 786436
  332.9 36.0 %all-to-all-start.3 = ((bf16[128,3,2048]{2,1,0:T(4,128)(2,1)}), bf16[128,3,2048]{2,1,0:T(4,128)(2,1)}, u32[]{:S(2)}, u32[]{:S(2)}) async-start(bf16[128,3,2048]{2,1,0:T(4,128)(2,1)} %reshape.384), calls=%async_computation.3 | async-start | bytes 4194304 | tf_op jit(solution)/shard_map/all_to_all | solution.py:207
  380.9 3.8 copy-start.3
Sparse Core Ops, SparseCore 0:
  11.0 65.5 all-gather.2
  78.7 38.0 all-gather.4
  124.0 83.4 all-reduce.1
where the time goes:
time: 399 us; the launch traced here: 397 us
  waiting for transfers between devices  203 us (51%)
  local copies, waits for them, and re-layouts  80.7 us (20%)
  other arithmetic  46.5 us (12%)
  starting transfers between devices  37.6 us (9%)
  matrix products  15 us (4%)
  between operations  14.2 us (4%)
    psum x1, waiting for transfers between devices, body(): mixed_all = lax.psum(head_terms, 'tp')  81.6 us
    all_to_all x1, waiting for transfers between devices, body(): lax.all_to_all(outgoing_pages, 'req', split_axis=0, concat_axis=0, tiled=...  50.5 us
    all_to_all x1, waiting for transfers between devices, body(): lax.all_to_all(packed, ('req', 'tp'), split_axis=0, concat_axis=1, tiled=...  46.3 us
    all_to_all x1, waiting for transfers between devices, body(): lax.all_to_all(expert_rows, ('req', 'tp'), split_axis=0, concat_axis=0, t...  24.4 us
    gather x4, local copies, waits for them, and re-layouts, body(): jnp.take(arrived_pages.reshape((req_count * capacity,) + page_shape), own...  16.8 us
    unnamed x35, local copies, waits for them, and re-layouts  11.9 us
    all_to_all x1, starting transfers between devices, body(): lax.all_to_all(send_rows, ('req', 'tp'), split_axis=0, concat_axis=0, til...  11.8 us
    concatenate x1, other arithmetic, body(): jnp.concatenate([split_halves(gate_weight.astype(jnp.bfloat16)), split_ha...  10.6 us
  transfers between devices with their start and end apart: 7, of which 4 were waited for; matrix products, arithmetic and copies ran while one was open for 24% of the time, Pallas kernels for 0%

commit v1 on v0

--- a/solution.py
+++ b/solution.py
@@ -167,7 +167,7 @@
     shard_rows = routes.shape[0]
     row_start = lane_index * shard_rows
     head_terms = jnp.dot(attended, server_out, preferred_element_type=jnp.float32)
-    mixed_all = lax.psum(head_terms, "tp")
+    mixed_all = lax.all_gather(head_terms, "tp").sum(axis=0)
     mixed_own = lax.dynamic_slice_in_dim(mixed_all, row_start, shard_rows, 0)
     residual_own = lax.dynamic_slice_in_dim(tokens_f32, row_start, shard_rows, 0) + mixed_own
     moe_own = rms_scale(residual_own, moe_gain).astype(jnp.bfloat16)

time: 399 us -> 424 us (1.063)
  waiting for transfers between devices: 203 us -> 229 us
  starting transfers between devices: 37.6 us -> 32.9 us
    all_gather x0 -> x1, waiting for transfers between devices: none -> 107 us  [body(): mixed_all = lax.all_gather(head_terms, 'tp').sum(axis=0)]
    psum x1 -> x0, waiting for transfers between devices: 81.6 us -> none  [body(): mixed_all = lax.psum(head_terms, 'tp')]
    all_to_all x1, starting transfers between devices: 11.8 us -> 7.08 us  [body(): lax.all_to_all(send_rows, ('req', 'tp'), split_axis=0, concat_axis=0, til...]
  transfers between devices with their start and end apart: 7 -> 7, of which waited for: 4 -> 4; matrix products, arithmetic and copies ran while one was open for 24% -> 22% of each run, Pallas kernels for 0% -> 0%
where the time goes in v1:
time: 424 us; the launch traced here: 422 us
  waiting for transfers between devices  229 us (54%)
  local copies, waits for them, and re-layouts  80.7 us (19%)
  other arithmetic  50.7 us (12%)
  starting transfers between devices  32.9 us (8%)
  matrix products  14.9 us (4%)
  between operations  14.2 us (3%)
    all_gather x1, waiting for transfers between devices, body(): mixed_all = lax.all_gather(head_terms, 'tp').sum(axis=0)  107 us
    all_to_all x1, waiting for transfers between devices, body(): lax.all_to_all(outgoing_pages, 'req', split_axis=0, concat_axis=0, tiled=...  50.5 us
    all_to_all x1, waiting for transfers between devices, body(): lax.all_to_all(packed, ('req', 'tp'), split_axis=0, concat_axis=1, tiled=...  46.3 us
    all_to_all x1, waiting for transfers between devices, body(): lax.all_to_all(expert_rows, ('req', 'tp'), split_axis=0, concat_axis=0, t...  24.4 us
    gather x4, local copies, waits for them, and re-layouts, body(): jnp.take(arrived_pages.reshape((req_count * capacity,) + page_shape), own...  16.8 us
    unnamed x35, local copies, waits for them, and re-layouts  11.9 us
    concatenate x1, other arithmetic, body(): jnp.concatenate([split_halves(gate_weight.astype(jnp.bfloat16)), split_ha...  10.6 us
    all_to_all x1, starting transfers between devices, body(): lax.all_to_all(packed, ('req', 'tp'), split_axis=0, concat_axis=1, tiled=...  10.2 us
  transfers between devices with their start and end apart: 7, of which 4 were waited for; matrix products, arithmetic and copies ran while one was open for 22% of the time, Pallas kernels for 0%

profile of v1, /device:TPU:1, one launch (start us, length us, event | category | flops | bytes accessed | tf_op | source)
XLA Modules:
  0.0 422.1 jit_solution(14751181766524881702)
XLA Ops:
  7.2 1.1 convert_element_type.109
  8.3 0.9 convert_element_type.110
  9.2 0.9 convert_element_type.111
  10.9 1.2 convert_reduce_fusion
  14.1 10.0 %gather_fusion = bf16[32,128,2,256]{3,2,1,0:T(2,128)(2,1)} fusion(bf16[8,128,2,256]{3,2,1,0:T(2,128)(2,1)S(1)} %copy-done.1, s32[1024]{0:T(1024)S(1)} %pad_clamp_fusion.2), kind=kCustom, calls=%fused_computation | custom fusion | bytes 8388736 | tf_op jit(solution)/shard_map/jit(_take)/gather | solution.py:125
  24.2 4.2 fusion
  28.4 8.1 %all-to-all-start.1 = ((bf16[16,2,128,2,256]{4,2,3,1,0:T(8,128)(2,1)}), bf16[16,2,128,2,256]{4,2,3,1,0:T(8,128)(2,1)}, u32[]{:S(2)}, u32[]{:S(2)}) async-start(bf16[16,2,128,2,256]{4,2,3,1,0:T(8,128)(2,1)} %fusion), calls=%async_computation.1 | async-start | bytes 8388608 | tf_op jit(solution)/shard_map/all_to_all | solution.py:131
  38.5 1.9 fusion.32
  40.5 1.9 compare_convert_fusion
  43.8 50.5 %all-to-all-done.1 = bf16[16,2,128,2,256]{4,2,3,1,0:T(8,128)(2,1)} async-done(((bf16[16,2,128,2,256]{4,2,3,1,0:T(8,128)(2,1)}), bf16[16,2,128,2,256]{4,2,3,1,0:T(8,128)(2,1)}, u32[]{:S(2)}, u32[]{:S(2)}) %all-to-all-start.1) | async-done | bytes 4194336 | tf_op jit(solution)/shard_map/all_to_all | solution.py:131
  94.4 4.2 %gather_fusion.1 = bf16[16,128,2,256]{3,1,2,0:T(8,128)(2,1)} fusion(bf16[32,128,2,256]{3,1,2,0:T(8,128)(2,1)} %bitcast.13, s32[1024]{0:T(1024)S(1)} %pad_clamp_fusion.1), kind=kCustom, calls=%fused_computation.1 | custom fusion | bytes 4194368 | tf_op jit(solution)/shard_map/jit(_take)/gather | solution.py:134
  98.6 4.5 %copy.135 = bf16[16,128,2,256]{1,0,3,2:T(8,128)(2,1)} copy(bf16[16,128,2,256]{3,1,2,0:T(8,128)(2,1)} %gather_fusion.1) | data formatting | bytes 4194304 | tf_op jit(solution)/shard_map/jit(_take)/gather | solution.py:134
  103.1 4.2 gather.28
  107.3 4.0 copy.136
  111.2 2.8 broadcast_select_fusion
  114.0 2.5 fusion.11
  121.3 2.5 fusion.43
  123.9 1.1 convert_element_type.115
  126.0 107.3 %all-gather.9.cloned.1.call-done = f32[1024,2048]{1,0:T(8,128)} async-done(((f32[128,2048]{1,0:T(8,128)}), f32[1024,2048]{1,0:T(8,128)}) %all-gather.9.cloned.1.call-update) | async-done | bytes 8388624 | tf_op jit(solution)/shard_map/all_gather | solution.py:170
  233.3 4.2 reduce_sum.119
  237.5 1.0 multiply_reduce_fusion.1
  238.5 1.3 convolution_convert_fusion.1
  239.8 2.4 broadcast_in_dim.156
  242.3 2.6 broadcast_in_dim.157
  244.9 7.1 %all-to-all-start.2 = ((bf16[128,3,2048]{2,1,0:T(4,128)(2,1)}), bf16[128,3,2048]{2,1,0:T(4,128)(2,1)}, u32[]{:S(2)}, u32[]{:S(2)}) async-start(bf16[128,3,2048]{2,1,0:T(4,128)(2,1)} %bitcast.104), calls=%async_computation.2 | async-start | bytes 4194304 | tf_op jit(solution)/shard_map/all_to_all | solution.py:198
  252.0 3.8 convert_element_type.113
  255.8 4.5 %reshape.372 = bf16[64,16,2,512]{3,2,1,0:T(2,128)(2,1)} reshape(bf16[64,16,1024]{2,1,0:T(8,128)(2,1)} %convert_element_type.113) | data formatting | bytes 4194304 | tf_op jit(solution)/shard_map/reshape | solution.py:32
  260.3 3.8 convert_element_type.114
  264.2 4.5 %reshape.373 = bf16[64,16,2,512]{3,2,1,0:T(2,128)(2,1)} reshape(bf16[64,16,1024]{2,1,0:T(8,128)(2,1)} %convert_element_type.114) | data formatting | bytes 4194304 | tf_op jit(solution)/shard_map/reshape | solution.py:32
  268.7 10.6 %pad_maximum_fusion = bf16[64,2,16,1024]{3,1,2,0:T(2,128)(2,1)} fusion(bf16[64,2,16,512]{3,1,2,0:T(2,128)(2,1)} %bitcast.106, bf16[64,2,16,512]{3,1,2,0:T(2,128)(2,1)} %bitcast.105), kind=kLoop, calls=%fused_computation.4 | loop fusion | flops 8388608 | bytes 8388608 | tf_op jit(solution)/shard_map/concatenate | solution.py:73
  279.2 5.6 %copy.126 = bf16[64,2,16,1024]{3,2,1,0:T(8,128)(2,1)} copy(bf16[64,2,16,1024]{3,1,2,0:T(2,128)(2,1)} %pad_maximum_fusion) | data formatting | bytes 8388608 | tf_op jit(solution)/shard_map/concatenate | solution.py:73
  284.8 10.2 %all-to-all-start = ((bf16[128,16,1024]{2,1,0:T(8,128)(2,1)}), bf16[128,16,1024]{2,1,0:T(8,128)(2,1)}, u32[]{:S(2)}, u32[]{:S(2)}) async-start(bf16[128,16,1024]{2,1,0:T(8,128)(2,1)} %bitcast.101), calls=%async_computation | async-start | bytes 8388608 | tf_op jit(solution)/shard_map/all_to_all | solution.py:80
  295.0 5.0 %reshape.383 = bf16[384,2048]{1,0:T(8,128)(2,1)} reshape(bf16[128,3,2048]{2,1,0:T(4,128)(2,1)} %all-to-all-done.2) | data formatting | bytes 3145728 | tf_op jit(solution)/shard_map/reshape | solution.py:199
  300.1 46.3 %all-to-all-done = bf16[128,16,1024]{2,1,0:T(8,128)(2,1)} async-done(((bf16[128,16,1024]{2,1,0:T(8,128)(2,1)}), bf16[128,16,1024]{2,1,0:T(8,128)(2,1)}, u32[]{:S(2)}, u32[]{:S(2)}) %all-to-all-start) | async-done | bytes 4194336 | tf_op jit(solution)/shard_map/all_to_all | solution.py:80
  346.4 4.4 %fusion.44 = f32[384,1024]{1,0:T(8,128)S(1)} fusion(bf16[384,2048]{1,0:T(8,128)(2,1)} %reshape.383, bf16[2048,1024]{1,0:T(8,128)(2,1)} %bitcast.20), kind=kOutput, calls=%fused_computation.128 | convolution fusion | flops 1610612736 | bytes 7340032 | tf_op jit(solution)/shard_map/dot_general | solution.py:200
  350.8 2.2 convolution_convert_fusion
  353.0 5.2 %reshape.384 = bf16[128,3,2048]{2,1,0:T(4,128)(2,1)} reshape(bf16[384,2048]{1,0:T(8,128)(2,1)} %convolution_convert_fusion) | data formatting | bytes 3145728 | tf_op jit(solution)/shard_map/reshape | solution.py:205
  358.2 7.5 %all-to-all-start.3 = ((bf16[128,3,2048]{2,1,0:T(4,128)(2,1)}), bf16[128,3,2048]{2,1,0:T(4,128)(2,1)}, u32[]{:S(2)}, u32[]{:S(2)}) async-start(bf16[128,3,2048]{2,1,0:T(4,128)(2,1)} %reshape.384), calls=%async_computation.3 | async-start | bytes 4194304 | tf_op jit(solution)/shard_map/all_to_all | solution.py:207
  366.2 0.9 slice_bitcast_fusion.8
  368.2 1.3 gather_fusion.3
  369.7 24.4 %all-to-all-done.3 = bf16[128,3,2048]{2,1,0:T(4,128)(2,1)} async-done(((bf16[128,3,2048]{2,1,0:T(4,128)(2,1)}), bf16[128,3,2048]{2,1,0:T(4,128)(2,1)}, u32[]{:S(2)}, u32[]{:S(2)}) %all-to-all-start.3) | async-done | bytes 1572896 | tf_op jit(solution)/shard_map/all_to_all | solution.py:207
  394.1 3.7 convert_add_fusion
  397.9 3.8 add.189
  401.6 2.9 gather_fusion.2
  404.5 0.9 fusion.9
  406.1 3.8 copy.167
  409.9 1.0 copy.168
  410.9 4.6 %copy.169 = bf16[1,2048,1024]{2,1,0:T(8,128)(2,1)} copy(bf16[1,2048,1024]{2,1,0:T(8,128)(2,1)} %bitcast.3) | data formatting | bytes 8388608
  (114 shorter events, 14.4 us)
Async XLA Ops:
  7.2 343.7 %copy-start = (bf16[1,512,2048]{2,1,0:T(8,128)(2,1)S(1)}, bf16[1,512,2048]{2,1,0:T(8,128)(2,1)}, u32[]{:S(2)}) copy-start(bf16[1,512,2048]{2,1,0:T(8,128)(2,1)} %param.32) | copy-start | bytes 6291460
  7.2 7.0 %copy-start.1 = (bf16[8,128,2,256]{3,2,1,0:T(2,128)(2,1)S(1)}, bf16[8,128,2,256]{3,2,1,0:T(2,128)(2,1)}, u32[]{:S(2)}) copy-start(bf16[8,128,2,256]{3,2,1,0:T(2,128)(2,1)} %param.34) | copy-start | bytes 3145732
  7.2 106.8 %all-gather.5.cloned.1.call-start = ((), (), s32[]{:S(2)}) async-start(), calls=%async_computation.4 | async-start | bytes 3342336 | tf_op jit(solution)/shard_map/all_gather | solution.py:68
  28.4 8.1 %copy-start.8 = (f32[256,128]{1,0:T(8,128)S(1)}, f32[256,128]{1,0:T(8,128)}, u32[]{:S(2)}) copy-start(f32[256,128]{1,0:T(8,128)} %param.29) | copy-start | bytes 393220
  28.4 8.9 %copy-start.13 = (s32[32]{0:T(128)S(1)}, s32[32]{0:T(128)}, u32[]{:S(2)}) copy-start(s32[32]{0:T(128)} %param.36) | copy-start | bytes 388
  28.4 9.0 %copy-start.14 = (s32[32]{0:T(128)S(1)}, s32[32]{0:T(128)}, u32[]{:S(2)}) copy-start(s32[32]{0:T(128)} %param.35) | copy-start | bytes 388
  28.4 14.8 %copy-start.2 = (bf16[128,2048]{1,0:T(8,128)(2,1)S(1)}, bf16[128,2048]{1,0:T(8,128)(2,1)}, u32[]{:S(2)}) copy-start(bf16[128,2048]{1,0:T(8,128)(2,1)} %param.21) | copy-start | bytes 1572868
  28.4 66.0 %all-to-all-start.1 = ((bf16[16,2,128,2,256]{4,2,3,1,0:T(8,128)(2,1)}), bf16[16,2,128,2,256]{4,2,3,1,0:T(8,128)(2,1)}, u32[]{:S(2)}, u32[]{:S(2)}) async-start(bf16[16,2,128,2,256]{4,2,3,1,0:T(8,128)(2,1)} %fusion), calls=%async_computation.1 | async-start | bytes 8388608 | tf_op jit(solution)/shard_map/all_to_all | solution.py:131
  36.5 84.8 %all-gather.7.cloned.1.call-start = ((), (), s32[]{:S(2)}) async-start(), calls=%async_computation.5 | async-start | bytes 1114112 | tf_op jit(solution)/shard_map/all_gather | solution.py:69
  37.2 196.1 %all-gather.9.cloned.1.call-start = ((), (), s32[]{:S(2)}) async-start(), calls=%async_computation.6 | async-start | bytes 9437184 | tf_op jit(solution)/shard_map/all_gather | solution.py:170
  111.2 2.8 copy-start.10
  114.0 4.2 %copy-start.11 = (f32[128]{0:T(128)S(1)}, f32[128]{0:T(128)}, u32[]{:S(2)}) copy-start(f32[128]{0:T(128)} %param.24) | copy-start | bytes 1540
  114.0 4.2 %copy-start.12 = (f32[128]{0:T(128)S(1)}, f32[128]{0:T(128)}, u32[]{:S(2)}) copy-start(f32[128]{0:T(128)} %param.23) | copy-start | bytes 1540
  116.5 0.8 copy-start.5
  118.2 1.6 copy-start.4
  121.3 3.6 copy-start.7
  233.3 5.2 %copy-start.9 = (f32[2048]{0:T(1024)S(1)}, f32[2048]{0:T(1024)}, u32[]{:S(2)}) copy-start(f32[2048]{0:T(1024)} %param.25) | copy-start | bytes 24580
  244.9 39.9 %all-to-all-start.2 = ((bf16[128,3,2048]{2,1,0:T(4,128)(2,1)}), bf16[128,3,2048]{2,1,0:T(4,128)(2,1)}, u32[]{:S(2)}, u32[]{:S(2)}) async-start(bf16[128,3,2048]{2,1,0:T(4,128)(2,1)} %bitcast.104), calls=%async_computation.2 | async-start | bytes 4194304 | tf_op jit(solution)/shard_map/all_to_all | solution.py:198
  284.8 61.5 %all-to-all-start = ((bf16[128,16,1024]{2,1,0:T(8,128)(2,1)}), bf16[128,16,1024]{2,1,0:T(8,128)(2,1)}, u32[]{:S(2)}, u32[]{:S(2)}) async-start(bf16[128,16,1024]{2,1,0:T(8,128)(2,1)} %bitcast.101), calls=%async_computation | async-start | bytes 8388608 | tf_op jit(solution)/shard_map/all_to_all | solution.py:80
  358.2 9.8 %copy-start.6 = (bf16[2048,64]{0,1:T(8,128)(2,1)S(1)}, bf16[2048,64]{0,1:T(8,128)(2,1)}, u32[]{:S(2)}) copy-start(bf16[2048,64]{0,1:T(8,128)(2,1)} %param.33) | copy-start | bytes 786436
  358.2 36.0 %all-to-all-start.3 = ((bf16[128,3,2048]{2,1,0:T(4,128)(2,1)}), bf16[128,3,2048]{2,1,0:T(4,128)(2,1)}, u32[]{:S(2)}, u32[]{:S(2)}) async-start(bf16[128,3,2048]{2,1,0:T(4,128)(2,1)} %reshape.384), calls=%async_computation.3 | async-start | bytes 4194304 | tf_op jit(solution)/shard_map/all_to_all | solution.py:207
  406.1 3.8 copy-start.3
Sparse Core Ops, SparseCore 0:
  11.0 65.5 all-gather.4
  78.7 38.0 all-gather.6
  124.0 109.2 all-gather.8
